TPU v7x, 32 devices: a whole 2x2x4 slice. The times are simulated.
32 devices in a mesh: wide: 8 (over z, y), narrow: 4 (over x, core).
Axes of the slice: x: 2, y: 2, z: 4, core: 2. Of those that a mesh axis runs over, the one named last changes fastest.
Arguments:
- frames: float32 [32768, 440], P(('wide', 'narrow')), may hold values from -8 to 8
- targets: float32 [32768, 2048], P(('wide', 'narrow')), may hold values from -7 to 7
- projection: float32 [32, 440, 512], P(('wide', 'narrow')), may hold values from -0.25 to 0.25
- phases: float32 [32, 512], P(('wide', 'narrow')), may hold values from 0 to 6.283185
- block_order: int32 [32], replicated, may hold values from 0 to 31, each once
Outputs:
- residual: float32 [32768, 2048], P(('wide', 'narrow'))
- weights: float32 [2, 512, 2048], replicated
Inputs may be any that keep to these rules, and one draw needn't show every extreme that they name: `block_order`: a permutation; steps use its first 2 entries.
All inputs are finite; a program needn't handle non-finite values.
Results may differ from a plain program's by a relative error of at most 0.0003.
Values sent between devices are 32-bit elements; how exact they have to be, the bound alone decides.
No kernel may reach another device: no remote copies, remote signals or barrier semaphores. Data moves between devices by JAX's collectives and lax.ppermute only.
A program may use at most 128 MiB of HBM per device.

v0:
```python
import jax
import jax.numpy as jnp
from jax import lax
from jax.sharding import PartitionSpec as P

STEPS = 2


def from_root(value, axis, source):
    kept = jnp.where(lax.axis_index(axis) == source, value, 0).astype(value.dtype)
    return lax.psum(kept, axis)


def features_of(frames, block_proj, block_phase):
    inner = jnp.dot(
        frames, block_proj, precision=lax.Precision.HIGHEST, preferred_element_type=jnp.float32
    )
    return jnp.sqrt(2.0 / block_proj.shape[1]) * jnp.cos(inner + block_phase[None, :])


def local_product(left, right):
    return jnp.dot(
        left.T, right, precision=lax.Precision.HIGHEST, preferred_element_type=jnp.float32
    )


def solve_block(gram_sum, cross_sum):
    width = gram_sum.shape[0]
    damping = 0.1 * jnp.trace(gram_sum) / width
    factor = jnp.linalg.cholesky(gram_sum + damping * jnp.eye(width, dtype=gram_sum.dtype))
    return jax.scipy.linalg.cho_solve((factor, True), cross_sum)


def per_device(frames, targets, projection, phases, block_order):
    feature_list = []
    for step_index in range(STEPS):
        block_proj, block_phase = (
            from_root(projection, ("wide", "narrow"), block_order[step_index]),
            from_root(phases, ("wide", "narrow"), block_order[step_index]),
        )
        feature_list.append(features_of(frames, block_proj[0], block_phase[0]))
    residual = targets
    solved = []
    for step_index in range(STEPS):
        feats = feature_list[step_index]
        cross_local = local_product(feats, residual)
        gram_sum = lax.psum(local_product(feats, feats), ("wide", "narrow"))
        cross_share = lax.psum_scatter(cross_local, "narrow", scatter_dimension=1, tiled=True)
        cross_share = lax.psum(cross_share, "wide")
        weight_share = solve_block(gram_sum, cross_share)
        weights = lax.all_gather(weight_share, "narrow", axis=1, tiled=True)
        residual = residual - jnp.dot(
            feats, weights, precision=lax.Precision.HIGHEST, preferred_element_type=jnp.float32
        )
        solved.append(weights)
    return (residual, jnp.stack(solved))


def solution(mesh):
    return jax.shard_map(
        per_device,
        mesh=mesh,
        in_specs=(
            P(("wide", "narrow"), None),
            P(("wide", "narrow"), None),
            P(("wide", "narrow"), None, None),
            P(("wide", "narrow"), None),
            P(),
        ),
        out_specs=(P(("wide", "narrow"), None), P()),
        check_vma=False,
    )
```

profile of v0, /device:TPU:0, one launch (start us, length us, event | category | flops | bytes accessed | tf_op | source)
XLA Modules:
  0.0 830.9 jit_solution(9541933310264790107)
XLA Ops:
  7.2 1.4 fusion.96
  9.9 2.6 select_bitcast_fusion
  12.6 42.1 %all-reduce.1 = (f32[512]{0:T(512)S(1)}, f32[512]{0:T(512)S(1)}) all-reduce(f32[512]{0:T(512)S(1)} %bitcast.143, f32[512]{0:T(512)S(1)} %bitcast.142), channel_id=1, replica_groups=mesh['wide'=8,'narrow'=4] {'wide','narrow'}, use_global_device_ids=true, to_apply=%region_1.2 | all-reduce | flops 1024 | bytes 8192 | tf_op jit(solution)/shard_map/psum | solution.py:11
  54.7 96.0 %all-reduce.15.cloned.1.call-done = (f32[440,512]{1,0:T(8,128)}, f32[440,512]{1,0:T(8,128)}) async-done(((f32[440,512]{1,0:T(8,128)}, f32[440,512]{1,0:T(8,128)}), (f32[440,512]{1,0:T(8,128)}, f32[440,512]{1,0:T(8,128)})) %all-reduce.15.cloned.1.call-update) | async-done | bytes 1802256 | tf_op jit(solution)/shard_map/psum | solution.py:11
  150.7 11.2 %cosine_multiply_fusion.1 = f32[512,1024]{1,0:T(8,128)S(1)} fusion(f32[440,512]{1,0:T(8,128)} %get-tuple-element.40, f32[1024,440]{0,1:T(8,128)S(1)} %copy-done, f32[512]{0:T(512)S(1)} %get-tuple-element.36), kind=kOutput, calls=%fused_computation.8 | convolution fusion | flops 2769289216 | bytes 4802560 | tf_op jit(solution)/shard_map/dot_general | solution.py:15
  162.0 13.4 %fusion.97 = f32[512,512]{0,1:T(8,128)} fusion(f32[512,1024]{1,0:T(8,128)S(1)} %cosine_multiply_fusion.1), kind=kOutput, calls=%fused_computation.185 | convolution fusion | flops 3221225472 | bytes 3145728 | tf_op jit(solution)/shard_map/dot_general | solution.py:22
  175.3 10.3 %cosine_multiply_fusion = f32[512,1024]{1,0:T(8,128)S(1)} fusion(f32[440,512]{1,0:T(8,128)S(1)} %copy-done.11, f32[1024,440]{0,1:T(8,128)S(1)} %copy-done, f32[512]{0:T(512)S(1)} %get-tuple-element.37), kind=kOutput, calls=%fused_computation.7 | convolution fusion | flops 2769289216 | bytes 4802560 | tf_op jit(solution)/shard_map/dot_general | solution.py:15
  185.7 1.4 copy-done.3
  187.1 4.5 fusion.99
  191.7 18.0 %fusion.98 = f32[512,2048]{1,0:T(8,128)} fusion(f32[512,1024]{1,0:T(8,128)} %copy-done.5, f32[1024,2048]{1,0:T(8,128)} %param.9), kind=kOutput, calls=%fused_computation.186 | convolution fusion | flops 12884901888 | bytes 14680064 | tf_op jit(solution)/shard_map/dot_general | solution.py:22
  210.2 115.3 %all-reduce.13.cloned.1.call-done = (f32[512,512]{0,1:T(8,128)}, f32[512,512]{0,1:T(8,128)}) async-done(((f32[512,512]{0,1:T(8,128)}, f32[512,512]{0,1:T(8,128)}), (f32[512,512]{0,1:T(8,128)}, f32[512,512]{0,1:T(8,128)})) %all-reduce.13.cloned.1.call-update) | async-done | bytes 2097168 | tf_op jit(solution)/shard_map/psum | solution.py:47
  325.5 2.0 select_reduce_fusion
  328.1 2.0 select_reduce_fusion.1
  330.7 1.8 select_add_fusion
  333.9 1.5 fusion.1
  336.4 11.7 %cholesky.286 = f32[128,128]{1,0:T(8,128)S(1)} custom-call(f32[128,128]{1,0:T(8,128)S(1)} %cholesky.426), custom_call_target="Cholesky" | custom-call | tf_op jit(solution)/shard_map/jit(cholesky)/cholesky | solution.py:30
  348.2 9.8 %custom-call.29 = f32[1,128,128]{1,2,0:T(8,128)S(1)} custom-call(f32[1,128,128]{2,1,0:T(8,128)S(1)} %get-tuple-element.67), custom_call_target="InvertDiagBlocksLowerTriangular" | custom-call | tf_op jit(solution)/shard_map/jit(cholesky)/cholesky | solution.py:30
  360.6 11.7 %cholesky.305 = f32[128,128]{1,0:T(8,128)S(1)} custom-call(f32[128,128]{1,0:T(8,128)S(1)} %cholesky.430), custom_call_target="Cholesky" | custom-call | tf_op jit(solution)/shard_map/jit(cholesky)/cholesky | solution.py:30
  372.4 10.0 %custom-call.30 = f32[1,128,128]{1,2,0:T(8,128)S(1)} custom-call(f32[1,128,128]{2,1,0:T(8,128)S(1)} %get-tuple-element.64), custom_call_target="InvertDiagBlocksLowerTriangular" | custom-call | tf_op jit(solution)/shard_map/jit(cholesky)/cholesky | solution.py:30
  383.9 11.7 %cholesky.326 = f32[128,128]{1,0:T(8,128)S(1)} custom-call(f32[128,128]{1,0:T(8,128)S(1)} %cholesky.435), custom_call_target="Cholesky" | custom-call | tf_op jit(solution)/shard_map/jit(cholesky)/cholesky | solution.py:30
  395.7 9.8 %custom-call.31 = f32[1,128,128]{1,2,0:T(8,128)S(1)} custom-call(f32[1,128,128]{2,1,0:T(8,128)S(1)} %get-tuple-element.61), custom_call_target="InvertDiagBlocksLowerTriangular" | custom-call | tf_op jit(solution)/shard_map/jit(cholesky)/cholesky | solution.py:30
  406.9 11.9 %cholesky.343 = f32[128,128]{1,0:T(8,128)S(1)} custom-call(f32[128,128]{1,0:T(8,128)S(1)} %convolution_subtract_fusion.19), custom_call_target="Cholesky" | custom-call | tf_op jit(solution)/shard_map/jit(cholesky)/cholesky | solution.py:30
  425.5 11.8 %while.4 = (s32[]{:T(128)}, f32[512,512]{1,0:T(8,128)}, s32[4,2]{0,1:T(2,128)S(1)}, f32[4,128,128]{2,1,0:T(8,128)S(1)}, s32[]{:T(128)}) while((s32[]{:T(128)}, f32[512,512]{1,0:T(8,128)}, s32[4,2]{0,1:T(2,128)S(1)}, f32[4,128,128]{2,1,0:T(8,128)S(1)}, s32[]{:T(128)}) %tuple.58), condition=%wide.while_cond, body=%wide.while_body.sunk | while | flops 2 | bytes 131189 | solution.py:31
  426.2 2.3 bitcast_dynamic-update-slice_fusion.4
  429.1 2.3 bitcast_dynamic-update-slice_fusion.4
  432.1 2.3 bitcast_dynamic-update-slice_fusion.4
  435.1 2.2 bitcast_dynamic-update-slice_fusion.4
  437.3 39.3 %custom-call.32 = f32[4,128,128]{1,2,0:T(8,128)S(1)} custom-call(f32[4,128,128]{2,1,0:T(8,128)S(1)} %get-tuple-element.18), custom_call_target="InvertDiagBlocksLowerTriangular" | custom-call | tf_op jit(solution)/shard_map/jit(_cho_solve)/triangular_solve | solution.py:31
  476.6 26.8 %all-reduce.9.cloned.1.call-done = f32[512,512]{1,0:T(8,128)} async-done(((f32[512,512]{1,0:T(8,128)}), f32[512,512]{1,0:T(8,128)}) %all-reduce.9.cloned.1.call-update) | async-done | bytes 1048592 | tf_op jit(solution)/shard_map/psum | solution.py:49
  508.4 1.6 convolution_subtract_fusion.13
  515.0 33.7 %all-gather.3.cloned.1.call-done = f32[512,2048]{1,0:T(8,128)} async-done(((f32[512,512]{1,0:T(8,128)}), f32[512,2048]{1,0:T(8,128)}) %all-gather.3.cloned.1.call-update) | async-done | bytes 4194320 | tf_op jit(solution)/shard_map/all_gather | solution.py:51
  548.8 16.9 %convolution_subtract_fusion.1 = f32[1024,2048]{1,0:T(8,128)S(1)} fusion(f32[1024,2048]{1,0:T(8,128)} %param.9, f32[512,1024]{1,0:T(8,128)} %copy-done.5, f32[512,2048]{1,0:T(8,128)} %all-gather.3.cloned.1.call-done), kind=kOutput, calls=%fused_computation.6 | convolution fusion | flops 12886999040 | bytes 23068672 | tf_op jit(solution)/shard_map/dot_general | solution.py:52
  565.7 3.4 copy-done.2
  569.1 17.2 %fusion.100 = f32[512,2048]{1,0:T(8,128)} fusion(f32[512,1024]{1,0:T(8,128)} %copy-done.3, f32[1024,2048]{1,0:T(8,128)S(1)} %convolution_subtract_fusion.1), kind=kOutput, calls=%fused_computation.188 | convolution fusion | flops 12884901888 | bytes 14680064 | tf_op jit(solution)/shard_map/dot_general | solution.py:22
  588.1 11.7 %cholesky.358 = f32[128,128]{1,0:T(8,128)S(1)} custom-call(f32[128,128]{1,0:T(8,128)S(1)} %cholesky.439), custom_call_target="Cholesky" | custom-call | tf_op jit(solution)/shard_map/jit(cholesky)/cholesky | solution.py:30
  599.9 9.8 %custom-call.33 = f32[1,128,128]{1,2,0:T(8,128)S(1)} custom-call(f32[1,128,128]{2,1,0:T(8,128)S(1)} %get-tuple-element.57), custom_call_target="InvertDiagBlocksLowerTriangular" | custom-call | tf_op jit(solution)/shard_map/jit(cholesky)/cholesky | solution.py:30
  612.3 11.7 %cholesky.377 = f32[128,128]{1,0:T(8,128)S(1)} custom-call(f32[128,128]{1,0:T(8,128)S(1)} %cholesky.443), custom_call_target="Cholesky" | custom-call | tf_op jit(solution)/shard_map/jit(cholesky)/cholesky | solution.py:30
  624.1 10.0 %custom-call.34 = f32[1,128,128]{1,2,0:T(8,128)S(1)} custom-call(f32[1,128,128]{2,1,0:T(8,128)S(1)} %get-tuple-element.54), custom_call_target="InvertDiagBlocksLowerTriangular" | custom-call | tf_op jit(solution)/shard_map/jit(cholesky)/cholesky | solution.py:30
  635.7 11.7 %cholesky.398 = f32[128,128]{1,0:T(8,128)S(1)} custom-call(f32[128,128]{1,0:T(8,128)S(1)} %cholesky.448), custom_call_target="Cholesky" | custom-call | tf_op jit(solution)/shard_map/jit(cholesky)/cholesky | solution.py:30
  647.4 9.8 %custom-call.35 = f32[1,128,128]{1,2,0:T(8,128)S(1)} custom-call(f32[1,128,128]{2,1,0:T(8,128)S(1)} %get-tuple-element.51), custom_call_target="InvertDiagBlocksLowerTriangular" | custom-call | tf_op jit(solution)/shard_map/jit(cholesky)/cholesky | solution.py:30
  658.7 11.7 %cholesky.415 = f32[128,128]{1,0:T(8,128)S(1)} custom-call(f32[128,128]{1,0:T(8,128)S(1)} %convolution_subtract_fusion.18), custom_call_target="Cholesky" | custom-call | tf_op jit(solution)/shard_map/jit(cholesky)/cholesky | solution.py:30
  676.2 8.1 while.5
  684.2 39.3 %custom-call.36 = f32[4,128,128]{1,2,0:T(8,128)S(1)} custom-call(f32[4,128,128]{2,1,0:T(8,128)S(1)} %get-tuple-element.19), custom_call_target="InvertDiagBlocksLowerTriangular" | custom-call | tf_op jit(solution)/shard_map/jit(_cho_solve)/triangular_solve | solution.py:31
  723.5 31.3 %all-reduce.11.cloned.1.call-done = f32[512,512]{1,0:T(8,128)} async-done(((f32[512,512]{1,0:T(8,128)}), f32[512,512]{1,0:T(8,128)}) %all-reduce.11.cloned.1.call-update) | async-done | bytes 1048592 | tf_op jit(solution)/shard_map/psum | solution.py:49
  754.9 1.5 fusion.34
  764.2 34.2 %all-gather.5.cloned.1.call-done = f32[512,2048]{1,0:T(8,128)} async-done(((f32[512,512]{1,0:T(8,128)}), f32[512,2048]{1,0:T(8,128)}) %all-gather.5.cloned.1.call-update) | async-done | bytes 4194320 | tf_op jit(solution)/shard_map/all_gather | solution.py:51
  798.4 8.1 pad_maximum_fusion
  806.5 17.1 %convolution_subtract_fusion = f32[1024,2048]{1,0:T(8,128)} fusion(f32[1024,2048]{1,0:T(8,128)} %copy-done.2, f32[512,1024]{1,0:T(8,128)S(1)} %copy-done.4, f32[512,2048]{1,0:T(8,128)S(1)} %copy-done.6), kind=kOutput, calls=%fused_computation.5 | convolution fusion | flops 12886999040 | bytes 23068672 | tf_op jit(solution)/shard_map/dot_general | solution.py:52
  (136 shorter events, 51.7 us)
Async XLA Ops:
  7.2 143.5 %copy-start = (f32[1024,440]{0,1:T(8,128)S(1)}, f32[1024,440]{0,1:T(8,128)}, u32[]{:S(2)}) copy-start(f32[1024,440]{0,1:T(8,128)} %param.8) | copy-start | bytes 5406724
  7.2 143.5 %all-reduce.15.cloned.1.call-start = ((), (), s32[]{:S(2)}) async-start(), calls=%async_computation.9 | async-start | bytes 3604480 | tf_op jit(solution)/shard_map/psum | solution.py:11
  9.9 2.7 copy-start.12
  12.6 312.9 %all-reduce.13.cloned.1.call-start = ((), (), s32[]{:S(2)}) async-start(), calls=%async_computation.8 | async-start | bytes 4194304 | tf_op jit(solution)/shard_map/psum | solution.py:47
  161.9 13.4 %copy-start.5 = (f32[512,1024]{1,0:T(8,128)}, f32[512,1024]{1,0:T(8,128)S(1)}, u32[]{:S(2)}) copy-start(f32[512,1024]{1,0:T(8,128)S(1)} %cosine_multiply_fusion.1) | copy-start | bytes 6291460
  162.0 13.4 %copy-start.11 = (f32[440,512]{1,0:T(8,128)S(1)}, f32[440,512]{1,0:T(8,128)}, u32[]{:S(2)}) copy-start(f32[440,512]{1,0:T(8,128)} %get-tuple-element.41) | copy-start | bytes 2703364
  185.7 1.4 copy-start.3
  191.6 233.8 %reduce-scatter.3.cloned.1.call-start = ((), (), s32[]{:S(2)}) async-start(), calls=%async_computation.2 | async-start | bytes 5242880 | tf_op jit(solution)/shard_map/reduce_scatter | solution.py:48
  209.7 293.7 %all-reduce.9.cloned.1.call-start = ((), (), s32[]{:S(2)}) async-start(), calls=%async_computation.3 | async-start | bytes 2097152 | tf_op jit(solution)/shard_map/psum | solution.py:49
  335.4 1.0 copy-start.8
  425.4 123.4 %all-gather.3.cloned.1.call-start = ((), (), s32[]{:S(2)}) async-start(), calls=%async_computation.4 | async-start | bytes 5242880 | tf_op jit(solution)/shard_map/all_gather | solution.py:51
  437.3 69.3 %copy-start.7 = (f32[512,512]{1,0:T(8,128)S(1)}, f32[512,512]{1,0:T(8,128)}, u32[]{:S(2)}) copy-start(f32[512,512]{1,0:T(8,128)} %get-tuple-element.187) | copy-start | bytes 3145732
  514.6 161.5 %reduce-scatter.5.cloned.1.call-start = ((), (), s32[]{:S(2)}) async-start(), calls=%async_computation.5 | async-start | bytes 5242880 | tf_op jit(solution)/shard_map/reduce_scatter | solution.py:48
  565.7 3.4 copy-start.2
  586.3 168.6 %all-reduce.11.cloned.1.call-start = ((), (), s32[]{:S(2)}) async-start(), calls=%async_computation.6 | async-start | bytes 2097152 | tf_op jit(solution)/shard_map/psum | solution.py:49
  587.1 1.0 copy-start.9
  676.1 122.3 %all-gather.5.cloned.1.call-start = ((), (), s32[]{:S(2)}) async-start(), calls=%async_computation.7 | async-start | bytes 5242880 | tf_op jit(solution)/shard_map/all_gather | solution.py:51
  754.9 3.2 copy-start.10
  798.4 8.1 copy-start.4
  798.4 8.1 copy-start.6
  806.5 17.2 %copy-start.1 = (f32[1024,440]{0,1:T(8,128)S(1)}, f32[1024,440]{0,1:T(8,128)}, u32[]{:S(2)}) copy-start(f32[1024,440]{0,1:T(8,128)} %param.8) | copy-start | bytes 5406724
Sparse Core Ops, SparseCore 0:
  14.0 136.6 all-reduce.14
  191.7 133.7 all-reduce.12
  328.6 43.2 reduce-scatter.2
  425.5 77.8 all-reduce.8
  514.7 34.0 all-gather.2
  586.4 44.4 reduce-scatter.4
  676.2 78.6 all-reduce.10
  764.3 34.0 all-gather.4
where the time goes:
time: 841 us; the launch traced here: 831 us
  waiting for transfers between devices  338 us (40%)
  other arithmetic  259 us (31%)
  matrix products  138 us (16%)
  blocking collectives  42.1 us (5%)
  local copies, waits for them, and re-layouts  29.9 us (4%)
  between operations  23 us (3%)
    another operation x30, other arithmetic, solve_block(): jnp.linalg.cholesky(gram_sum + damping * jnp.eye(width, dtype=gram_sum.dt...  159 us
    psum x1, waiting for transfers between devices, per_device(): gram_sum = lax.psum(local_product(feats, feats), ('wide', 'narrow'))  115 us
    psum x1, waiting for transfers between devices, from_root(): return lax.psum(kept, axis)  96 us
    another operation x7, other arithmetic, solve_block(): return jax.scipy.linalg.cho_solve((factor, True), cross_sum)  82.2 us
    all_gather x2, waiting for transfers between devices, per_device(): weights = lax.all_gather(weight_share, 'narrow', axis=1, tiled=True)  68 us
    psum x2, waiting for transfers between devices, per_device(): cross_share = lax.psum(cross_share, 'wide')  58.2 us
    dot_general x4, matrix products, local_product(): jnp.dot(left.T, right, precision=lax.Precision.HIGHEST, preferred_element...  53.1 us
    psum x1, blocking collectives, from_root(): return lax.psum(kept, axis)  42.1 us
  transfers between devices with their start and end apart: 8, of which 6 were waited for; matrix products, arithmetic and copies ran while one was open for 36% of the time, Pallas kernels for 0%

commit v1 on v0

--- a/solution.py
+++ b/solution.py
@@ -44,7 +44,9 @@
     for step_index in range(STEPS):
         feats = feature_list[step_index]
         cross_local = local_product(feats, residual)
-        gram_sum = lax.psum(local_product(feats, feats), ("wide", "narrow"))
+        gram_sum = local_product(feats, feats)
+        for mesh_axis in ("narrow", "wide"):
+            gram_sum = lax.psum(gram_sum, mesh_axis)
         cross_share = lax.psum_scatter(cross_local, "narrow", scatter_dimension=1, tiled=True)
         cross_share = lax.psum(cross_share, "wide")
         weight_share = solve_block(gram_sum, cross_share)

time: 841 us -> 993 us (1.18)
  waiting for transfers between devices: 338 us -> 499 us
    psum x2, waiting for transfers between devices: 58.2 us -> 211 us  [per_device(): cross_share = lax.psum(cross_share, 'wide')]
    reduce_scatter x2, waiting for transfers between devices: 0.02 us -> 92.2 us  [per_device(): lax.psum_scatter(cross_local, 'narrow', scatter_dimension=1, tiled=True)]
    psum x1, waiting for transfers between devices: 115 us -> 32.6 us  [per_device(): gram_sum = lax.psum(gram_sum, mesh_axis)]
    another operation x30 -> x29, other arithmetic: 159 us -> 158 us  [solve_block(): jnp.linalg.cholesky(gram_sum + damping * jnp.eye(width, dtype=gram_sum.dt...]
  transfers between devices with their start and end apart: 8 -> 8, of which waited for: 6 -> 8; matrix products, arithmetic and copies ran while one was open for 36% -> 2% of each run, Pallas kernels for 0% -> 0%
where the time goes in v1:
time: 993 us; the launch traced here: 983 us
  waiting for transfers between devices  499 us (50%)
  other arithmetic  260 us (26%)
  matrix products  132 us (13%)
  blocking collectives  42.1 us (4%)
  local copies, waits for them, and re-layouts  25.3 us (3%)
  between operations  22.9 us (2%)
    psum x2, waiting for transfers between devices, per_device(): cross_share = lax.psum(cross_share, 'wide')  211 us
    another operation x29, other arithmetic, solve_block(): jnp.linalg.cholesky(gram_sum + damping * jnp.eye(width, dtype=gram_sum.dt...  158 us
    psum x1, waiting for transfers between devices, from_root(): return lax.psum(kept, axis)  95.9 us
    reduce_scatter x2, waiting for transfers between devices, per_device(): lax.psum_scatter(cross_local, 'narrow', scatter_dimension=1, tiled=True)  92.2 us
    another operation x7, other arithmetic, solve_block(): return jax.scipy.linalg.cho_solve((factor, True), cross_sum)  81 us
    all_gather x2, waiting for transfers between devices, per_device(): weights = lax.all_gather(weight_share, 'narrow', axis=1, tiled=True)  67.4 us
    dot_general x4, matrix products, local_product(): jnp.dot(left.T, right, precision=lax.Precision.HIGHEST, preferred_element...  53.2 us
    psum x1, blocking collectives, from_root(): return lax.psum(kept, axis)  42.1 us
  transfers between devices with their start and end apart: 8, of which 8 were waited for; matrix products, arithmetic and copies ran while one was open for 2% of the time, Pallas kernels for 0%

profile of v1, /device:TPU:0, one launch (start us, length us, event | category | flops | bytes accessed | tf_op | source)
XLA Modules:
  0.0 983.0 jit_solution(13588131492743810394)
XLA Ops:
  9.9 2.6 select_bitcast_fusion
  12.6 42.1 %all-reduce.1 = (f32[512]{0:T(512)S(1)}, f32[512]{0:T(512)S(1)}) all-reduce(f32[512]{0:T(512)S(1)} %bitcast.143, f32[512]{0:T(512)S(1)} %bitcast.142), channel_id=1, replica_groups=mesh['wide'=8,'narrow'=4] {'wide','narrow'}, use_global_device_ids=true, to_apply=%region_1.2 | all-reduce | flops 1024 | bytes 8192 | tf_op jit(solution)/shard_map/psum | solution.py:11
  54.8 95.9 %all-reduce.11.cloned.1.call-done = (f32[440,512]{1,0:T(8,128)}, f32[440,512]{1,0:T(8,128)}) async-done(((f32[440,512]{1,0:T(8,128)}, f32[440,512]{1,0:T(8,128)}), (f32[440,512]{1,0:T(8,128)}, f32[440,512]{1,0:T(8,128)})) %all-reduce.11.cloned.1.call-update) | async-done | bytes 1802256 | tf_op jit(solution)/shard_map/psum | solution.py:11
  150.7 11.2 %cosine_multiply_fusion.1 = f32[512,1024]{1,0:T(8,128)S(1)} fusion(f32[440,512]{1,0:T(8,128)} %get-tuple-element.38, f32[1024,440]{0,1:T(8,128)S(1)} %copy-done, f32[512]{0:T(512)S(1)} %get-tuple-element.36), kind=kOutput, calls=%fused_computation.8 | convolution fusion | flops 2769289216 | bytes 4802560 | tf_op jit(solution)/shard_map/dot_general | solution.py:15
  162.0 13.4 %fusion.97 = f32[512,512]{0,1:T(8,128)} fusion(f32[512,1024]{1,0:T(8,128)S(1)} %cosine_multiply_fusion.1), kind=kOutput, calls=%fused_computation.185 | convolution fusion | flops 3221225472 | bytes 3145728 | tf_op jit(solution)/shard_map/dot_general | solution.py:22
  175.4 10.3 %cosine_multiply_fusion = f32[512,1024]{1,0:T(8,128)S(1)} fusion(f32[440,512]{1,0:T(8,128)S(1)} %copy-done.9, f32[1024,440]{0,1:T(8,128)S(1)} %copy-done, f32[512]{0:T(512)S(1)} %get-tuple-element.37), kind=kOutput, calls=%fused_computation.7 | convolution fusion | flops 2769289216 | bytes 4802560 | tf_op jit(solution)/shard_map/dot_general | solution.py:15
  187.1 4.6 fusion.99
  191.7 18.0 %fusion.98 = f32[512,2048]{1,0:T(8,128)} fusion(f32[512,1024]{1,0:T(8,128)} %copy-done.5, f32[1024,2048]{1,0:T(8,128)} %param.9), kind=kOutput, calls=%fused_computation.186 | convolution fusion | flops 12884901888 | bytes 14680064 | tf_op jit(solution)/shard_map/dot_general | solution.py:22
  209.8 32.6 %all-reduce.17.cloned.1.call-done = (f32[512,512]{0,1:T(8,128)}, f32[512,512]{0,1:T(8,128)}) async-done(((f32[512,512]{0,1:T(8,128)}, f32[512,512]{0,1:T(8,128)}), (f32[512,512]{0,1:T(8,128)}, f32[512,512]{0,1:T(8,128)})) %all-reduce.17.cloned.1.call-update) | async-done | bytes 2097168 | tf_op jit(solution)/shard_map/psum | solution.py:49
  242.4 47.6 %reduce-scatter.3.cloned.1.call-done = f32[512,512]{1,0:T(8,128)} async-done(((f32[512,2048]{1,0:T(8,128)}), f32[512,512]{1,0:T(8,128)}) %reduce-scatter.3.cloned.1.call-update) | async-done | bytes 1048592 | tf_op jit(solution)/shard_map/reduce_scatter | solution.py:50
  290.5 105.4 %all-reduce.15.cloned.1.call-done = (f32[512,512]{1,0:T(8,128)}, f32[512,512]{0,1:T(8,128)}) async-done(((f32[512,512]{1,0:T(8,128)}, f32[512,512]{0,1:T(8,128)}), (f32[512,512]{1,0:T(8,128)}, f32[512,512]{0,1:T(8,128)})) %all-reduce.15.cloned.1.call-update) | async-done | bytes 2097168 | tf_op jit(solution)/shard_map/psum | solution.py:51
  395.9 1.9 select_reduce_fusion.1
  401.2 1.4 fusion.1
  402.6 11.7 %cholesky.286 = f32[128,128]{1,0:T(8,128)S(1)} custom-call(f32[128,128]{1,0:T(8,128)S(1)} %cholesky.426), custom_call_target="Cholesky" | custom-call | tf_op jit(solution)/shard_map/jit(cholesky)/cholesky | solution.py:30
  414.4 9.8 custom-call.29
  425.0 11.7 %cholesky.305 = f32[128,128]{1,0:T(8,128)S(1)} custom-call(f32[128,128]{1,0:T(8,128)S(1)} %cholesky.430), custom_call_target="Cholesky" | custom-call | tf_op jit(solution)/shard_map/jit(cholesky)/cholesky | solution.py:30
  436.7 10.0 %custom-call.30 = f32[1,128,128]{1,2,0:T(8,128)S(1)} custom-call(f32[1,128,128]{2,1,0:T(8,128)S(1)} %get-tuple-element.68), custom_call_target="InvertDiagBlocksLowerTriangular" | custom-call | tf_op jit(solution)/shard_map/jit(cholesky)/cholesky | solution.py:30
  447.4 11.7 %cholesky.326 = f32[128,128]{1,0:T(8,128)S(1)} custom-call(f32[128,128]{1,0:T(8,128)S(1)} %cholesky.435), custom_call_target="Cholesky" | custom-call | tf_op jit(solution)/shard_map/jit(cholesky)/cholesky | solution.py:30
  459.9 9.8 custom-call.31
  470.3 11.7 %cholesky.343 = f32[128,128]{1,0:T(8,128)S(1)} custom-call(f32[128,128]{1,0:T(8,128)S(1)} %convolution_subtract_fusion.19), custom_call_target="Cholesky" | custom-call | tf_op jit(solution)/shard_map/jit(cholesky)/cholesky | solution.py:30
  486.2 8.5 while.4
  486.9 1.4 bitcast_dynamic-update-slice_fusion.4
  489.0 1.4 bitcast_dynamic-update-slice_fusion.4
  491.1 1.4 bitcast_dynamic-update-slice_fusion.4
  493.3 1.4 bitcast_dynamic-update-slice_fusion.4
  494.7 39.3 %custom-call.32 = f32[4,128,128]{1,2,0:T(8,128)S(1)} custom-call(f32[4,128,128]{2,1,0:T(8,128)S(1)} %get-tuple-element.18), custom_call_target="InvertDiagBlocksLowerTriangular" | custom-call | tf_op jit(solution)/shard_map/jit(_cho_solve)/triangular_solve | solution.py:31
  539.0 1.6 convolution_subtract_fusion.13
  545.6 33.4 %all-gather.3.cloned.1.call-done = f32[512,2048]{1,0:T(8,128)} async-done(((f32[512,512]{1,0:T(8,128)}), f32[512,2048]{1,0:T(8,128)}) %all-gather.3.cloned.1.call-update) | async-done | bytes 4194320 | tf_op jit(solution)/shard_map/all_gather | solution.py:53
  579.0 16.9 %convolution_subtract_fusion.1 = f32[1024,2048]{1,0:T(8,128)S(1)} fusion(f32[1024,2048]{1,0:T(8,128)} %param.9, f32[512,1024]{1,0:T(8,128)} %copy-done.5, f32[512,2048]{1,0:T(8,128)} %all-gather.3.cloned.1.call-done), kind=kOutput, calls=%fused_computation.6 | convolution fusion | flops 12886999040 | bytes 23068672 | tf_op jit(solution)/shard_map/dot_general | solution.py:54
  595.9 3.4 copy-done.2
  599.3 17.2 %fusion.100 = f32[512,2048]{1,0:T(8,128)} fusion(f32[512,1024]{1,0:T(8,128)} %copy-done.3, f32[1024,2048]{1,0:T(8,128)S(1)} %convolution_subtract_fusion.1), kind=kOutput, calls=%fused_computation.188 | convolution fusion | flops 12884901888 | bytes 14680064 | tf_op jit(solution)/shard_map/dot_general | solution.py:22
  616.6 44.5 %reduce-scatter.5.cloned.1.call-done = f32[512,512]{1,0:T(8,128)} async-done(((f32[512,2048]{1,0:T(8,128)}), f32[512,512]{1,0:T(8,128)}) %reduce-scatter.5.cloned.1.call-update) | async-done | bytes 1048592 | tf_op jit(solution)/shard_map/reduce_scatter | solution.py:50
  661.4 105.8 %all-reduce.13.cloned.1.call-done = (f32[512,512]{1,0:T(8,128)}, f32[512,512]{0,1:T(8,128)}) async-done(((f32[512,512]{1,0:T(8,128)}, f32[512,512]{0,1:T(8,128)}), (f32[512,512]{1,0:T(8,128)}, f32[512,512]{0,1:T(8,128)})) %all-reduce.13.cloned.1.call-update) | async-done | bytes 2097168 | tf_op jit(solution)/shard_map/psum | solution.py:51
  767.1 1.9 select_reduce_fusion
  772.4 1.4 fusion
  773.9 11.7 %cholesky.358 = f32[128,128]{1,0:T(8,128)S(1)} custom-call(f32[128,128]{1,0:T(8,128)S(1)} %cholesky.439), custom_call_target="Cholesky" | custom-call | tf_op jit(solution)/shard_map/jit(cholesky)/cholesky | solution.py:30
  786.3 9.8 custom-call.33
  796.9 11.7 %cholesky.377 = f32[128,128]{1,0:T(8,128)S(1)} custom-call(f32[128,128]{1,0:T(8,128)S(1)} %cholesky.443), custom_call_target="Cholesky" | custom-call | tf_op jit(solution)/shard_map/jit(cholesky)/cholesky | solution.py:30
  809.3 10.0 %custom-call.34 = f32[1,128,128]{1,2,0:T(8,128)S(1)} custom-call(f32[1,128,128]{2,1,0:T(8,128)S(1)} %get-tuple-element.58), custom_call_target="InvertDiagBlocksLowerTriangular" | custom-call | tf_op jit(solution)/shard_map/jit(cholesky)/cholesky | solution.py:30
  820.0 11.7 %cholesky.398 = f32[128,128]{1,0:T(8,128)S(1)} custom-call(f32[128,128]{1,0:T(8,128)S(1)} %cholesky.448), custom_call_target="Cholesky" | custom-call | tf_op jit(solution)/shard_map/jit(cholesky)/cholesky | solution.py:30
  832.4 9.8 custom-call.35
  842.8 11.9 %cholesky.415 = f32[128,128]{1,0:T(8,128)S(1)} custom-call(f32[128,128]{1,0:T(8,128)S(1)} %convolution_subtract_fusion.18), custom_call_target="Cholesky" | custom-call | tf_op jit(solution)/shard_map/jit(cholesky)/cholesky | solution.py:30
  858.2 7.9 while.5
  866.1 39.3 %custom-call.36 = f32[4,128,128]{1,2,0:T(8,128)S(1)} custom-call(f32[4,128,128]{2,1,0:T(8,128)S(1)} %get-tuple-element.19), custom_call_target="InvertDiagBlocksLowerTriangular" | custom-call | tf_op jit(solution)/shard_map/jit(_cho_solve)/triangular_solve | solution.py:31
  910.4 1.6 convolution_subtract_fusion.11
  916.5 33.9 %all-gather.5.cloned.1.call-done = f32[512,2048]{1,0:T(8,128)} async-done(((f32[512,512]{1,0:T(8,128)}), f32[512,2048]{1,0:T(8,128)}) %all-gather.5.cloned.1.call-update) | async-done | bytes 4194320 | tf_op jit(solution)/shard_map/all_gather | solution.py:53
  950.5 8.1 pad_maximum_fusion
  958.6 17.1 %convolution_subtract_fusion = f32[1024,2048]{1,0:T(8,128)} fusion(f32[1024,2048]{1,0:T(8,128)} %copy-done.2, f32[512,1024]{1,0:T(8,128)S(1)} %copy-done.4, f32[512,2048]{1,0:T(8,128)S(1)} %copy-done.6), kind=kOutput, calls=%fused_computation.5 | convolution fusion | flops 12886999040 | bytes 23068672 | tf_op jit(solution)/shard_map/dot_general | solution.py:54
  (132 shorter events, 48.4 us)
Async XLA Ops:
  7.2 143.5 %copy-start = (f32[1024,440]{0,1:T(8,128)S(1)}, f32[1024,440]{0,1:T(8,128)}, u32[]{:S(2)}) copy-start(f32[1024,440]{0,1:T(8,128)} %param.8) | copy-start | bytes 5406724
  7.2 143.5 %all-reduce.11.cloned.1.call-start = ((), (), s32[]{:S(2)}) async-start(), calls=%async_computation.6 | async-start | bytes 3604480 | tf_op jit(solution)/shard_map/psum | solution.py:11
  9.9 2.7 copy-start.10
  12.6 229.8 %all-reduce.17.cloned.1.call-start = ((), (), s32[]{:S(2)}) async-start(), calls=%async_computation.9 | async-start | bytes 4194304 | tf_op jit(solution)/shard_map/psum | solution.py:49
  161.9 13.4 %copy-start.5 = (f32[512,1024]{1,0:T(8,128)}, f32[512,1024]{1,0:T(8,128)S(1)}, u32[]{:S(2)}) copy-start(f32[512,1024]{1,0:T(8,128)S(1)} %cosine_multiply_fusion.1) | copy-start | bytes 6291460
  162.0 13.4 %copy-start.9 = (f32[440,512]{1,0:T(8,128)S(1)}, f32[440,512]{1,0:T(8,128)}, u32[]{:S(2)}) copy-start(f32[440,512]{1,0:T(8,128)} %get-tuple-element.39) | copy-start | bytes 2703364
  185.7 1.4 copy-start.3
  191.7 98.3 %reduce-scatter.3.cloned.1.call-start = ((), (), s32[]{:S(2)}) async-start(), calls=%async_computation.2 | async-start | bytes 5242880 | tf_op jit(solution)/shard_map/reduce_scatter | solution.py:50
  209.7 186.1 %all-reduce.15.cloned.1.call-start = ((), (), s32[]{:S(2)}) async-start(), calls=%async_computation.8 | async-start | bytes 4194304 | tf_op jit(solution)/shard_map/psum | solution.py:51
  290.0 289.0 %all-gather.3.cloned.1.call-start = ((), (), s32[]{:S(2)}) async-start(), calls=%async_computation.3 | async-start | bytes 5242880 | tf_op jit(solution)/shard_map/all_gather | solution.py:53
  398.4 2.7 copy-start.7
  545.1 116.0 %reduce-scatter.5.cloned.1.call-start = ((), (), s32[]{:S(2)}) async-start(), calls=%async_computation.4 | async-start | bytes 5242880 | tf_op jit(solution)/shard_map/reduce_scatter | solution.py:50
  595.9 3.4 copy-start.2
  616.5 150.6 %all-reduce.13.cloned.1.call-start = ((), (), s32[]{:S(2)}) async-start(), calls=%async_computation.7 | async-start | bytes 4194304 | tf_op jit(solution)/shard_map/psum | solution.py:51
  661.1 289.3 %all-gather.5.cloned.1.call-start = ((), (), s32[]{:S(2)}) async-start(), calls=%async_computation.5 | async-start | bytes 5242880 | tf_op jit(solution)/shard_map/all_gather | solution.py:53
  769.7 2.7 copy-start.8
  950.5 8.1 copy-start.4
  950.5 8.1 copy-start.6
  958.6 17.1 %copy-start.1 = (f32[1024,440]{0,1:T(8,128)S(1)}, f32[1024,440]{0,1:T(8,128)}, u32[]{:S(2)}) copy-start(f32[1024,440]{0,1:T(8,128)} %param.8) | copy-start | bytes 5406724
Sparse Core Ops, SparseCore 0:
  14.0 136.6 all-reduce.10
  191.8 50.5 all-reduce.16
  245.5 44.4 reduce-scatter.2
  293.5 102.3 all-reduce.14
  545.2 33.7 all-gather.2
  616.6 44.4 reduce-scatter.4
  664.8 102.3 all-reduce.12
  916.7 33.7 all-gather.4
